TPU v7x, 512 devices: a whole 4x4x16 slice. The times are simulated.
512 devices in a mesh: wide: 64 (over y, z), narrow: 8 (over x, core).
Axes of the slice: x: 4, y: 4, z: 16, core: 2. Of those that a mesh axis runs over, the one named last changes fastest.
Arguments:
- panel: float32 [8, 16777216], P(None, ('wide', 'narrow')), may hold values from -0.25 to 0.25
- signs: int32 [16777216], P(('wide', 'narrow')), may hold values from -1 to 1, as said below
- samples: int32 [65536], P(('wide', 'narrow')), may hold values from 0 to 16777215, as said below
Outputs:
- sketch: float32 [8, 65536], P(None, ('wide', 'narrow'))
Inputs may be any that keep to these rules, and one draw needn't show every extreme that they name: `signs`: every entry is +1 or -1. `samples`: for every k, entries 128 * k to 128 * (k + 1) - 1 are distinct, increasing, and lie among rows 32768 * k to 32768 * (k + 1) - 1.
All inputs are finite; a program needn't handle non-finite values.
Results may differ from a plain program's by a relative error of at most 0.000071.
Values sent between devices are 32-bit elements; how exact they have to be, the bound alone decides.
A program may use at most 64 MiB of HBM per device.

v0:
```python
import math

import jax
import jax.numpy as jnp
from jax import lax
from jax.sharding import PartitionSpec as P


def from_partner(block, axis, bit):
    count = lax.axis_size(axis)
    route = []
    for low in range(count):
        high = low | 1 << bit
        if high != low and high < count:
            route += [(low, high), (high, low)]
    return lax.ppermute(block, axis, route)


def parity_sign(left, right, nbits):
    count = (left & 0) + (right & 0)
    for level in range(nbits):
        count = count + (left >> level & 1) * (right >> level & 1)
    return (1 - 2 * (count % 2)).astype(jnp.float32)


def sylvester(order):
    nbits = max(order.bit_length() - 1, 0)
    index = jnp.arange(order, dtype=jnp.int32)
    return parity_sign(index[:, None], index[None, :], nbits)


def local_transform(values):
    cols, rows = values.shape
    inner = min(128, rows)
    outer = rows // inner
    blocks = values.reshape(cols, outer, inner)
    blocks = jnp.einsum("cab,bj->caj", blocks, sylvester(inner), precision=lax.Precision.HIGHEST)
    blocks = jnp.einsum("cab,ai->cib", blocks, sylvester(outer), precision=lax.Precision.HIGHEST)
    return blocks.reshape(cols, rows)


def narrow_section(values):
    n_narrow = lax.axis_size("narrow")
    narrow_bits = n_narrow.bit_length() - 1
    narrow_me = lax.axis_index("narrow")
    for level in range(narrow_bits):
        partner = from_partner(values, "narrow", level)
        upper = narrow_me >> level & 1 == 1
        values = jnp.where(upper, partner - values, values + partner)
    return values


def wide_section(values):
    cols, rows = values.shape
    n_wide = lax.axis_size("wide")
    arranged = values.reshape(cols, n_wide, rows // n_wide)
    received = lax.all_to_all(arranged, "wide", split_axis=1, concat_axis=1, tiled=True)
    return jnp.einsum("ij,cjp->cip", sylvester(n_wide), received, precision=lax.Precision.HIGHEST)


def per_device(panel, signs, samples):
    cols, rows = panel.shape
    samp = samples.shape[0]
    n_wide = lax.axis_size("wide")
    n_narrow = lax.axis_size("narrow")
    total_samples = samp * n_wide * n_narrow
    values = local_transform(panel * signs.astype(jnp.float32)[None, :])
    offsets = samples % rows
    mixed = wide_section(narrow_section(values))
    returned = lax.all_to_all(mixed, "wide", split_axis=1, concat_axis=1, tiled=True).reshape(
        cols, rows
    )
    chosen = jnp.take(returned, offsets, axis=1)
    return chosen * jnp.float32(1.0 / math.sqrt(total_samples))


def solution(mesh):
    in_specs = (P(None, ("wide", "narrow")), P(("wide", "narrow")), P(("wide", "narrow")))
    out_specs = P(None, ("wide", "narrow"))
    return jax.shard_map(
        per_device, mesh=mesh, in_specs=in_specs, out_specs=out_specs, check_vma=False
    )
```

profile of v0, /device:TPU:1, one launch (start us, length us, event | category | flops | bytes accessed | tf_op | source)
XLA Modules:
  0.0 213.6 jit_solution(2722790776690722395)
XLA Ops:
  0.0 0.0 copy-start
  0.1 0.9 convert_element_type.13
  1.0 1.3 multiply_bitcast_fusion
  2.3 1.2 fusion
  3.5 1.3 convolution_bitcast_fusion.1
  4.8 0.6 copy.19
  5.4 8.7 %collective-permute-start = (f32[8,32768]{1,0:T(8,128)S(1)}, f32[8,32768]{1,0:T(8,128)S(1)}, u32[]{:S(2)}, u32[]{:S(2)}) collective-permute-start(f32[8,32768]{1,0:T(8,128)S(1)} %bitcast.27), channel_id=1, source_target_pairs={{0,1},{1,0},{2,3},{3,2},{4,5},{5,4},{6,7},{7,6},{8,9},{9,8},{10,11... | collective-permute-start | bytes 3145736 | tf_op jit(solution)/shard_map/ppermute | solution.py:16
  14.2 2.3 %collective-permute-done = f32[8,32768]{1,0:T(8,128)S(1)} collective-permute-done((f32[8,32768]{1,0:T(8,128)S(1)}, f32[8,32768]{1,0:T(8,128)S(1)}, u32[]{:S(2)}, u32[]{:S(2)}) %collective-permute-start) | collective-permute-done | bytes 1048608 | tf_op jit(solution)/shard_map/ppermute | solution.py:16
  16.4 0.6 add_select_fusion.2
  17.1 1.9 collective-permute-start.1
  19.0 24.3 %collective-permute-done.1 = f32[8,32768]{1,0:T(8,128)S(1)} collective-permute-done((f32[8,32768]{1,0:T(8,128)S(1)}, f32[8,32768]{1,0:T(8,128)S(1)}, u32[]{:S(2)}, u32[]{:S(2)}) %collective-permute-start.1) | collective-permute-done | bytes 1048608 | tf_op jit(solution)/shard_map/ppermute | solution.py:16
  43.3 0.1 add_select_fusion.1
  43.4 1.9 collective-permute-start.2
  45.4 25.0 %collective-permute-done.2 = f32[8,32768]{1,0:T(8,128)S(1)} collective-permute-done((f32[8,32768]{1,0:T(8,128)S(1)}, f32[8,32768]{1,0:T(8,128)S(1)}, u32[]{:S(2)}, u32[]{:S(2)}) %collective-permute-start.2) | collective-permute-done | bytes 1048608 | tf_op jit(solution)/shard_map/ppermute | solution.py:16
  70.3 1.1 add_select_fusion
  71.4 13.1 %all-to-all-start = ((f32[8,64,512]{2,0,1:T(8,128)}), f32[8,64,512]{2,0,1:T(8,128)S(1)}, u32[]{:S(2)}, u32[]{:S(2)}) async-start(f32[8,64,512]{2,0,1:T(8,128)} %bitcast.4), calls=%async_computation | async-start | bytes 2097152 | tf_op jit(solution)/shard_map/all_to_all | solution.py:57
  84.6 48.6 %all-to-all-done = f32[8,64,512]{2,0,1:T(8,128)S(1)} async-done(((f32[8,64,512]{2,0,1:T(8,128)}), f32[8,64,512]{2,0,1:T(8,128)S(1)}, u32[]{:S(2)}, u32[]{:S(2)}) %all-to-all-start) | async-done | bytes 1048608 | tf_op jit(solution)/shard_map/all_to_all | solution.py:57
  133.2 1.7 convolution_bitcast_fusion
  135.0 1.6 copy.7
  136.5 11.6 %all-to-all-start.1 = ((f32[8,64,512]{2,0,1:T(8,128)}), f32[8,64,512]{2,0,1:T(8,128)S(1)}, u32[]{:S(2)}, u32[]{:S(2)}) async-start(f32[8,64,512]{2,0,1:T(8,128)} %copy.7), calls=%async_computation.1 | async-start | bytes 2097152 | tf_op jit(solution)/shard_map/all_to_all | solution.py:70
  148.2 0.0 copy-done
  148.2 50.2 %all-to-all-done.1 = f32[8,64,512]{2,0,1:T(8,128)S(1)} async-done(((f32[8,64,512]{2,0,1:T(8,128)}), f32[8,64,512]{2,0,1:T(8,128)S(1)}, u32[]{:S(2)}, u32[]{:S(2)}) %all-to-all-start.1) | async-done | bytes 1048608 | tf_op jit(solution)/shard_map/all_to_all | solution.py:70
  198.4 8.1 %copy.8 = f32[8,64,512]{0,2,1:T(8,128)} copy(f32[8,64,512]{2,0,1:T(8,128)S(1)} %all-to-all-done.1) | data formatting | bytes 2097152 | tf_op jit(solution)/shard_map/all_to_all | solution.py:70
  206.4 6.4 %gather_fusion = f32[128,8]{1,0:T(8,128)S(1)} fusion(f32[8,32768]{0,1:T(8,128)} %bitcast.26, s32[1024]{0:T(1024)S(1)} %pad_clamp_fusion), kind=kCustom, calls=%fused_computation | custom fusion | bytes 8704 | tf_op jit(solution)/shard_map/jit(_take)/gather | solution.py:73
  212.9 0.1 multiply_bitcast_fusion.1
  212.9 0.7 copy.9
  (13 shorter events, 0.1 us)
Async XLA Ops:
  0.0 148.2 %copy-start = (s32[128]{0:T(128)S(1)}, s32[128]{0:T(128)}, u32[]{:S(2)}) copy-start(s32[128]{0:T(128)} %param.5) | copy-start | bytes 1540
  5.4 11.0 %collective-permute-start = (f32[8,32768]{1,0:T(8,128)S(1)}, f32[8,32768]{1,0:T(8,128)S(1)}, u32[]{:S(2)}, u32[]{:S(2)}) collective-permute-start(f32[8,32768]{1,0:T(8,128)S(1)} %bitcast.27), channel_id=1, source_target_pairs={{0,1},{1,0},{2,3},{3,2},{4,5},{5,4},{6,7},{7,6},{8,9},{9,8},{10,11... | collective-permute-start | bytes 3145736 | tf_op jit(solution)/shard_map/ppermute | solution.py:16
  17.1 26.2 %collective-permute-start.1 = (f32[8,32768]{1,0:T(8,128)S(1)}, f32[8,32768]{1,0:T(8,128)S(1)}, u32[]{:S(2)}, u32[]{:S(2)}) collective-permute-start(f32[8,32768]{1,0:T(8,128)S(1)} %add_select_fusion.2), channel_id=1, source_target_pairs={{0,2},{2,0},{1,3},{3,1},{4,6},{6,4},{5,7},{7,5},{8,10},{10,8},{9,1... | collective-permute-start | bytes 3145736 | tf_op jit(solution)/shard_map/ppermute | solution.py:16
  43.4 26.9 %collective-permute-start.2 = (f32[8,32768]{1,0:T(8,128)S(1)}, f32[8,32768]{1,0:T(8,128)S(1)}, u32[]{:S(2)}, u32[]{:S(2)}) collective-permute-start(f32[8,32768]{1,0:T(8,128)S(1)} %add_select_fusion.1), channel_id=1, source_target_pairs={{0,4},{4,0},{1,5},{5,1},{2,6},{6,2},{3,7},{7,3},{8,12},{12,8},{9,1... | collective-permute-start | bytes 3145736 | tf_op jit(solution)/shard_map/ppermute | solution.py:16
  71.4 61.8 %all-to-all-start = ((f32[8,64,512]{2,0,1:T(8,128)}), f32[8,64,512]{2,0,1:T(8,128)S(1)}, u32[]{:S(2)}, u32[]{:S(2)}) async-start(f32[8,64,512]{2,0,1:T(8,128)} %bitcast.4), calls=%async_computation | async-start | bytes 2097152 | tf_op jit(solution)/shard_map/all_to_all | solution.py:57
  136.5 61.8 %all-to-all-start.1 = ((f32[8,64,512]{2,0,1:T(8,128)}), f32[8,64,512]{2,0,1:T(8,128)S(1)}, u32[]{:S(2)}, u32[]{:S(2)}) async-start(f32[8,64,512]{2,0,1:T(8,128)} %copy.7), calls=%async_computation.1 | async-start | bytes 2097152 | tf_op jit(solution)/shard_map/all_to_all | solution.py:70
where the time goes:
time: 217 us; the launch traced here: 214 us
  waiting for transfers between devices  150 us (69%)
  starting transfers between devices  37.3 us (17%)
  local copies, waits for them, and re-layouts  17.3 us (8%)
  other arithmetic  4.24 us (2%)
  matrix products  4.19 us (2%)
    ppermute x3, waiting for transfers between devices, from_partner(): return lax.ppermute(block, axis, route)  51.5 us
    all_to_all x1, waiting for transfers between devices, per_device(): lax.all_to_all(mixed, 'wide', split_axis=1, concat_axis=1, tiled=True)  50.2 us
    all_to_all x1, waiting for transfers between devices, wide_section(): lax.all_to_all(arranged, 'wide', split_axis=1, concat_axis=1, tiled=True)  48.6 us
    all_to_all x1, starting transfers between devices, wide_section(): lax.all_to_all(arranged, 'wide', split_axis=1, concat_axis=1, tiled=True)  13.1 us
    ppermute x3, starting transfers between devices, from_partner(): return lax.ppermute(block, axis, route)  12.6 us
    all_to_all x1, starting transfers between devices, per_device(): lax.all_to_all(mixed, 'wide', split_axis=1, concat_axis=1, tiled=True)  11.6 us
    all_to_all x1, local copies, waits for them, and re-layouts, per_device(): lax.all_to_all(mixed, 'wide', split_axis=1, concat_axis=1, tiled=True)  8.06 us
    gather x1, local copies, waits for them, and re-layouts, per_device(): chosen = jnp.take(returned, offsets, axis=1)  6.41 us
  transfers between devices with their start and end apart: 5, of which 5 were waited for; matrix products, arithmetic and copies ran while one was open for 0% of the time, Pallas kernels for 0%

commit v1 on v0

v1 whole, which is shorter than its diff:
```python
import functools
import math

import jax
import jax.numpy as jnp
from jax import lax
from jax.experimental import pallas as pl
from jax.experimental.pallas import tpu as pltpu
from jax.sharding import PartitionSpec as P

MESH = pl.DeviceIdType.MESH
NX, NY, NZ, NC = 4, 4, 16, 2
LANES = 128
LAG = 6


def parity(value, bits):
    shift = 1
    while shift * 2 < bits:
        shift *= 2
    while shift >= 1:
        value = value ^ (value >> shift)
        shift //= 2
    return value & 1


def hadamard(rows, columns, bits):
    left = lax.broadcasted_iota(jnp.int32, (rows, columns), 0)
    right = lax.broadcasted_iota(jnp.int32, (rows, columns), 1)
    odd = parity(left & right & ((1 << bits) - 1), bits)
    return (1 - 2 * odd).astype(jnp.float32).astype(jnp.bfloat16)


def split(values):
    high = values.astype(jnp.bfloat16)
    low = (values - high.astype(jnp.float32)).astype(jnp.bfloat16)
    return high, low


def signed(odd, values):
    return jnp.where(odd == 0, values, -values)


def kernel(
    scale, panel, signs, samples, out,
    mixed, sent, came, table, idx_y, idx_x, idx_all, pick, part, zsum, zcame, rows_out, rows_in,
    x_send, x_recv, iz_send, iz_recv, iy_send, iy_recv, ix_send, ix_recv, ia_send, ia_recv,
    q_send, q_recv, z_send, z_recv, r_send, r_recv, local,
):
    wide = lax.axis_index("wide")
    narrow = lax.axis_index("narrow")
    y, z = wide // NZ, wide % NZ
    x, core = narrow // NC, narrow % NC
    role0 = core == 0
    p = jnp.where(role0, x, y)
    q = jnp.where(role0, y, x)
    outer = panel.shape[1] // LANES

    def device(dx, dy, dz, dc):
        return (dy * NZ + dz, dx * NC + dc)

    def by_role(dp, dq, dz):
        return device(jnp.where(role0, dp, dq), jnp.where(role0, dq, dp), dz, core)

    def remote(src, dst, send, recv, to):
        return pltpu.make_async_remote_copy(
            src_ref=src, dst_ref=dst, send_sem=send, recv_sem=recv, device_id=to, device_id_type=MESH
        )

    def wait_bytes(ref, sem):
        pltpu.make_async_copy(ref, ref, sem).wait()

    barrier = pltpu.get_barrier_semaphore()

    def greet(to):
        pl.semaphore_signal(barrier, inc=1, device_id=to, device_id_type=MESH)

    @pl.loop(1, NZ)
    def _(step):
        greet(device(x, y, lax.rem(z + step, NZ), core))

    @pl.loop(1, NX * NC)
    def _(step):
        greet((wide, lax.rem(narrow + step, NX * NC)))

    for dy in range(1, NY):
        for dc in range(NC):
            greet(device(x, lax.rem(y + dy, NY), z, dc))

    h_lanes = hadamard(2 * LANES, LANES, 7)

    @pl.loop(0, outer // 8)
    def _(step):
        for sub in range(8):
            a = step * 8 + sub
            lanes = pl.ds(pl.multiple_of(a * LANES, LANES), LANES)
            row = signs[pl.ds(a, 1), :].astype(jnp.float32)
            mixed[pl.ds(pl.multiple_of(a * 8, 8), 8), :] = panel[:, lanes] * row

    @pl.loop(0, 8)
    def _(step):
        rows = pl.ds(pl.multiple_of(step * outer, outer), outer)
        high, low = split(mixed[rows, :])
        both = jnp.concatenate([high, low], axis=1)
        mixed[rows, :] = jnp.dot(both, h_lanes, preferred_element_type=jnp.float32)

    pl.semaphore_wait(barrier, NX * NC - 1 + (NY - 1) * NC + NZ - 1)

    def z_order(step):
        shift = jnp.where(step % 2 == 1, (step + 1) // 2, NZ - step // 2)
        return lax.rem(z + NZ // 2 + shift, NZ)

    idx_y[y, z] = samples[...]

    @pl.loop(0, NZ - 1)
    def _(step):
        remote(samples, idx_y.at[y, z], iz_send, iz_recv, device(x, y, z_order(step), core)).start()

    h_rows = hadamard(outer, outer, outer.bit_length() - 1)
    for j in range(8):
        high, low = split(mixed[pl.ds(j, outer, stride=8), :])
        both = jnp.concatenate([high, low], axis=1)
        done = jnp.dot(h_rows, both, preferred_element_type=jnp.float32)
        sent[j] = done[:, :LANES] + done[:, LANES:]
        if j < 4:
            to, slot = device(j, y, z, 0), x * NC + core
            mine = (core == 0) & (x == j)
        else:
            to, slot = device(x, j - 4, z, 1), y * NC + core
            mine = (core == 1) & (y == j - 4)

        @pl.when(mine)
        def _():
            pltpu.make_async_copy(sent.at[j], came.at[slot], local.at[0]).start()

        @pl.when(jnp.logical_not(mine))
        def _():
            remote(sent.at[j], came.at[slot], x_send, x_recv, to).start()

    wait_bytes(idx_y.at[0, pl.ds(0, NZ - 1)], iz_recv)
    keep = pltpu.make_async_copy(idx_y.at[y], idx_x.at[x], local.at[1])
    keep.start()
    for step in range(1, 4):
        to = device(x, lax.rem(y + step, NY), z, core)
        remote(idx_y.at[y], idx_y.at[y], iy_send, iy_recv, to).start()
        to = device(lax.rem(x + step, NX), y, z, core)
        remote(idx_y.at[y], idx_x.at[x], ix_send, ix_recv, to).start()
    keep.wait()
    wait_bytes(idx_y.at[pl.ds(0, 3)], iy_recv)
    wait_bytes(idx_y.at[pl.ds(0, 3)], ix_recv)
    for j in range(8):
        if j < 4:
            source, to, slot = idx_y, device(j, y, z, 0), x * NC + core
            mine = (core == 0) & (x == j)
        else:
            source, to, slot = idx_x, device(x, j - 4, z, 1), y * NC + core
            mine = (core == 1) & (y == j - 4)

        @pl.when(mine)
        def _():
            pltpu.make_async_copy(source, idx_all.at[slot], local.at[2]).start()

        @pl.when(jnp.logical_not(mine))
        def _():
            remote(source, idx_all.at[slot], ia_send, ia_recv, to).start()

    wait_bytes(came.at[0], local.at[0])
    wait_bytes(came.at[pl.ds(0, 7)], x_recv)

    @pl.loop(0, outer // 8)
    def _(step):
        rows = pl.ds(pl.multiple_of(step * 8, 8), 8)
        values = [came[m, rows, :] for m in range(8)]
        for level in range(3):
            half = 1 << level
            for m in range(8):
                if not m & half:
                    first, second = values[m], values[m | half]
                    values[m], values[m | half] = first + second, first - second
        for m in range(8):
            table[m, rows, :] = values[m]

    wait_bytes(idx_all.at[0], local.at[2])
    wait_bytes(idx_all.at[pl.ds(0, 7)], ia_recv)

    sublane = lax.broadcasted_iota(jnp.int32, (8, LANES), 0)

    def choose(step):
        to_z = z_order(step)

        @pl.loop(0, 4)
        def _(turn):
            to_q = lax.rem(q + 1 + turn, 4)

            @pl.loop(0, 8)
            def _(m):
                offset = jnp.broadcast_to(idx_all[m, to_q, to_z], (8, LANES)) & (outer * LANES - 1)
                lane = offset & (LANES - 1)
                key = (offset >> 7) - sublane
                found = jnp.zeros((8, LANES), jnp.float32)
                for i in range(outer // 8):
                    there = jnp.take_along_axis(
                        table[m, 8 * i : 8 * i + 8, :], lane, axis=1, mode="promise_in_bounds"
                    )
                    found = jnp.where(key == 8 * i, there, found)
                pick[to_z, turn, pl.ds(m, 1), :] = jnp.sum(found, axis=0, keepdims=True)

            @pl.when(turn < 3)
            def _():
                remote(
                    pick.at[to_z, turn], part.at[to_z, q], q_send, q_recv.at[to_z], by_role(p, to_q, z)
                ).start()

        part[to_z, q] = pick[to_z, 3]

    def pass_on(step):
        to_z = z_order(step)
        wait_bytes(part.at[0, pl.ds(0, 3)], q_recv.at[to_z])
        total = signed(parity(q & 0, 2), part[to_z, 0])
        for other in range(1, 4):
            total = total + signed(parity(q & other, 2), part[to_z, other])

        @pl.when(step < NZ - 1)
        def _():
            zsum[to_z] = total
            remote(zsum.at[to_z], zcame.at[z], z_send, z_recv, by_role(p, q, to_z)).start()

        @pl.when(step == NZ - 1)
        def _():
            zcame[z] = total

    @pl.loop(0, NZ)
    def _(step):
        choose(step)

        @pl.when(step >= LAG)
        def _():
            pass_on(step - LAG)

    @pl.loop(NZ - LAG, NZ)
    def _(step):
        pass_on(step)

    wait_bytes(zcame.at[pl.ds(0, NZ - 1)], z_recv)
    total = zcame[0]
    for other in range(1, NZ):
        total = total + signed(parity(z & other, 4), zcame[other])
    total = total * scale
    slot = core * 4 + p
    for m in range(8):
        rows_out[m] = total[m : m + 1, :]
    for m in range(8):
        to = device(jnp.where(role0, m // 2, x), jnp.where(role0, y, m // 2), z, m % 2)
        mine = (p == m // 2) & (core == m % 2)

        @pl.when(mine)
        def _():
            pltpu.make_async_copy(rows_out.at[m], rows_in.at[slot], local.at[3]).start()

        @pl.when(jnp.logical_not(mine))
        def _():
            remote(rows_out.at[m], rows_in.at[slot], r_send, r_recv, to).start()

    wait_bytes(rows_in.at[0], local.at[3])
    wait_bytes(rows_in.at[pl.ds(0, 7)], r_recv)
    for j in range(8):
        out[j : j + 1, :] = rows_in[j]

    wait_bytes(sent.at[pl.ds(0, 7)], x_send)
    wait_bytes(idx_y.at[0, pl.ds(0, NZ - 1)], iz_send)
    wait_bytes(idx_y.at[pl.ds(0, 3)], iy_send)
    wait_bytes(idx_y.at[pl.ds(0, 3)], ix_send)
    wait_bytes(idx_all.at[pl.ds(0, 7)], ia_send)
    wait_bytes(pick.at[pl.ds(0, 12)], q_send)
    wait_bytes(zsum.at[pl.ds(0, NZ - 1)], z_send)
    wait_bytes(rows_out.at[pl.ds(0, 7)], r_send)


def per_device(panel, signs, samples):
    cols, rows = panel.shape
    samp = samples.shape[0]
    n_wide, n_narrow = lax.axis_size("wide"), lax.axis_size("narrow")
    scale = 1.0 / math.sqrt(samp * n_wide * n_narrow)
    outer = rows // LANES
    dma = pltpu.SemaphoreType.DMA
    vmem = pl.BlockSpec(memory_space=pltpu.VMEM)
    f32, i32 = jnp.float32, jnp.int32
    return pl.pallas_call(
        functools.partial(kernel, scale),
        out_shape=jax.ShapeDtypeStruct((cols, samp), f32),
        in_specs=[vmem] * 3,
        out_specs=vmem,
        scratch_shapes=[
            pltpu.VMEM((cols * outer, LANES), f32),
            pltpu.VMEM((8, outer, LANES), f32),
            pltpu.VMEM((8, outer, LANES), f32),
            pltpu.VMEM((8, outer, LANES), f32),
            pltpu.VMEM((NY, NZ, 1, LANES), i32),
            pltpu.VMEM((NX, NZ, 1, LANES), i32),
            pltpu.VMEM((8, 4, NZ, 1, LANES), i32),
            pltpu.VMEM((NZ, 4, 8, LANES), f32),
            pltpu.VMEM((NZ, 4, 8, LANES), f32),
            pltpu.VMEM((NZ, 8, LANES), f32),
            pltpu.VMEM((NZ, 8, LANES), f32),
            pltpu.VMEM((8, 1, LANES), f32),
            pltpu.VMEM((8, 1, LANES), f32),
            dma, dma, dma, dma, dma, dma, dma, dma, dma, dma,
            dma, dma((NZ,)), dma, dma, dma, dma, dma((4,)),
        ],
        compiler_params=pltpu.CompilerParams(collective_id=0, has_side_effects=True),
    )(panel, signs.reshape(outer, LANES), samples.reshape(1, samp))


def solution(mesh):
    in_specs = (P(None, ("wide", "narrow")), P(("wide", "narrow")), P(("wide", "narrow")))
    out_specs = P(None, ("wide", "narrow"))
    return jax.shard_map(
        per_device, mesh=mesh, in_specs=in_specs, out_specs=out_specs, check_vma=False
    )
```

time: 217 us -> 103 us (0.47); the launches traced: 214 us -> 102 us
  waiting for transfers between devices: 150 us -> 0 us
  Pallas kernels: 0 us -> 101 us
  starting transfers between devices: 37.3 us -> 0 us
  local copies, waits for them, and re-layouts: 17.3 us -> 1.28 us
  other arithmetic: 4.24 us -> 0 us
  matrix products: 4.19 us -> 0 us
    pallas_call x0 -> x1, Pallas kernels: none -> 101 us  [per_device(): pl.pallas_call(functools.partial(kernel, scale), out_shape=jax.ShapeDtype...]
    all_to_all x2 -> x0, waiting for transfers between devices: 98.8 us -> none  [the longest x1 50.2 us: per_device(): lax.all_to_all(mixed, 'wide', split_axis=1, concat_axis=1, tiled=True)]
    ppermute x3 -> x0, waiting for transfers between devices: 51.5 us -> none  [from_partner(): return lax.ppermute(block, axis, route)]
    all_to_all x2 -> x0, starting transfers between devices: 24.7 us -> none  [the longest x1 13.1 us: wide_section(): lax.all_to_all(arranged, 'wide', split_axis=1, concat_axis=1, tiled=True)]
    ppermute x3 -> x0, starting transfers between devices: 12.6 us -> none  [from_partner(): return lax.ppermute(block, axis, route)]
    all_to_all x1 -> x0, local copies, waits for them, and re-layouts: 8.06 us -> none  [per_device(): lax.all_to_all(mixed, 'wide', split_axis=1, concat_axis=1, tiled=True)]
    gather x1 -> x0, local copies, waits for them, and re-layouts: 6.41 us -> none  [per_device(): chosen = jnp.take(returned, offsets, axis=1)]
    dot_general x3 -> x0, matrix products: 4.19 us -> none  [the longest x1 1.73 us: wide_section(): jnp.einsum('ij,cjp->cip', sylvester(n_wide), received, precision=lax.Prec...]
  transfers between devices with their start and end apart: 5 -> 0, of which waited for: 5 -> 0; matrix products, arithmetic and copies ran while one was open for 0% -> 0% of each run, Pallas kernels for 0% -> 0%
where the time goes in v1:
time: 103 us; the launch traced here: 102 us
  Pallas kernels  101 us (98%)
  local copies, waits for them, and re-layouts  1.28 us (1%)
    pallas_call x1, Pallas kernels, per_device(): pl.pallas_call(functools.partial(kernel, scale), out_shape=jax.ShapeDtype...  101 us

profile of v1, /device:TPU:1, one launch (start us, length us, event | category | flops | bytes accessed | tf_op | source)
XLA Modules:
  0.0 102.5 jit_solution(10337168923172273897)
XLA Ops:
  0.0 101.2 %shard_map.37 = f32[8,128]{1,0:T(8,128)} custom-call(f32[8,32768]{1,0:T(8,128)} %panel.1, s32[256,128]{1,0:T(8,128)} %bitcast.2, s32[1,128]{1,0:T(1,128)} %bitcast.3), custom_call_target="tpu_custom_call" | custom-call | tf_op jit(solution)/shard_map/pallas_call | solution.py:288
  101.2 1.3 %copy.5 = f32[8,128]{1,0:T(8,128)} copy(f32[8,128]{1,0:T(8,128)} %shard_map.37) | data formatting | bytes 8192

commit v2 on v1

v2 whole, which is shorter than its diff:
```python
import functools
import math

import jax
import jax.numpy as jnp
from jax import lax
from jax.experimental import pallas as pl
from jax.experimental.pallas import tpu as pltpu
from jax.sharding import PartitionSpec as P

MESH = pl.DeviceIdType.MESH
NX, NY, NZ, NC = 4, 4, 16, 2
LANES = 128
CHUNKS = 4
EARLY = 5


def parity(value, bits):
    shift = 1
    while shift * 2 < bits:
        shift *= 2
    while shift >= 1:
        value = value ^ (value >> shift)
        shift //= 2
    return value & 1


def hadamard(rows, columns, bits):
    left = lax.broadcasted_iota(jnp.int32, (rows, columns), 0)
    right = lax.broadcasted_iota(jnp.int32, (rows, columns), 1)
    odd = parity(left & right & ((1 << bits) - 1), bits)
    return (1 - 2 * odd).astype(jnp.float32).astype(jnp.bfloat16)


def split(values):
    high = values.astype(jnp.bfloat16)
    low = (values - high.astype(jnp.float32)).astype(jnp.bfloat16)
    return high, low


def signed(odd, values):
    return jnp.where(odd == 0, values, -values)


def kernel(
    scale, panel_hbm, signs_hbm, samples, out,
    panel, signs, mixed, sent, came, table, crossed, idx_z, idx_all, pick, zcame, rows_out, rows_in,
    load_sem, ring_send, up_recv, down_recv, x_send, x_recv, q_send, q_recv,
    i_send, i_recv, z_send, z_recv, r_send, r_recv,
):
    wide = lax.axis_index("wide")
    narrow = lax.axis_index("narrow")
    y, z = wide >> 4, wide & (NZ - 1)
    x, core = narrow >> 1, narrow & 1
    role0 = core == 0
    p = jnp.where(role0, x, y)
    q = jnp.where(role0, y, x)
    outer = signs_hbm.shape[0]
    rows_in_chunk = outer // CHUNKS

    def device(dx, dy, dz, dc):
        return (dy * NZ + dz, dx * NC + dc)

    def by_role(dp, dq, dz):
        return device(jnp.where(role0, dp, dq), jnp.where(role0, dq, dp), dz, core)

    def remote(src, dst, send, recv, to):
        return pltpu.make_async_remote_copy(
            src_ref=src, dst_ref=dst, send_sem=send, recv_sem=recv, device_id=to, device_id_type=MESH
        )

    def deliver(mine, src, dst, send, recv, to):
        @pl.when(mine)
        def _():
            pltpu.make_async_copy(src, dst, recv).start()

        @pl.when(jnp.logical_not(mine))
        def _():
            remote(src, dst, send, recv, to).start()

    def wait_bytes(ref, sem):
        pltpu.make_async_copy(ref, ref, sem).wait()

    def loads(chunk):
        lanes = pl.ds(chunk * rows_in_chunk * LANES, rows_in_chunk * LANES)
        rows = pl.ds(chunk * rows_in_chunk, rows_in_chunk)
        return (
            pltpu.make_async_copy(panel_hbm.at[:, lanes], panel.at[:, lanes], load_sem.at[chunk, 0]),
            pltpu.make_async_copy(signs_hbm.at[rows], signs.at[rows], load_sem.at[chunk, 1]),
        )

    for chunk in range(CHUNKS):
        for load in loads(chunk):
            load.start()

    barrier = pltpu.get_barrier_semaphore()

    def greet(to):
        pl.semaphore_signal(barrier, inc=1, device_id=to, device_id_type=MESH)

    above, below = (z + 1) & (NZ - 1), (z - 1) & (NZ - 1)
    greet(device(x, y, above, core))
    greet(device(x, y, below, core))

    @pl.loop(1, NX * NY * NC)
    def _(step):
        other = (narrow + y * NX * NC + step) & (NX * NY * NC - 1)
        greet(device((other >> 1) & 3, other >> 3, z, other & 1))

    h_lanes = hadamard(2 * LANES, LANES, 7)
    for chunk in range(CHUNKS):
        for load in loads(chunk):
            load.wait()
        flipped = []
        for sub in range(rows_in_chunk):
            a = chunk * rows_in_chunk + sub
            row = jnp.broadcast_to(signs[pl.ds(a, 1), :], (8, LANES)).astype(jnp.float32)
            flipped.append(panel[:, a * LANES : (a + 1) * LANES] * row)
        high, low = split(jnp.concatenate(flipped, axis=0))
        both = jnp.concatenate([high, low], axis=1)
        mixed[chunk * rows_in_chunk * 8 : (chunk + 1) * rows_in_chunk * 8, :] = jnp.dot(
            both, h_lanes, preferred_element_type=jnp.float32
        )
    h_rows = hadamard(outer, outer, outer.bit_length() - 1)

    pl.semaphore_wait(barrier, NX * NY * NC + 1)

    up, down = device(x, y, above, core), device(x, y, below, core)
    idx_z[z] = samples[...]

    def ring_up(step):
        row = (z - step) & (NZ - 1)
        src = samples if step == 0 else idx_z.at[row]
        return remote(src, idx_z.at[row], ring_send, up_recv.at[step], up)

    def ring_down(step):
        row = (z + step) & (NZ - 1)
        src = samples if step == 0 else idx_z.at[row]
        return remote(src, idx_z.at[row], ring_send, down_recv.at[step], down)

    def ring(step):
        ring_up(step - 1).wait_recv()
        if step < NZ // 2:
            ring_up(step).start()
            ring_down(step - 1).wait_recv()
            if step < NZ // 2 - 1:
                ring_down(step).start()

    ring_up(0).start()
    ring_down(0).start()

    for j in range(8):
        high, low = split(mixed[pl.ds(j, outer, stride=8), :])
        both = jnp.concatenate([high, low], axis=1)
        done = jnp.dot(h_rows, both, preferred_element_type=jnp.float32)
        sent[j] = done[:, :LANES] + done[:, LANES:]
        if j < 4:
            to, slot = device(j, y, z, 0), x * NC + core
            mine = (core == 0) & (x == j)
        else:
            to, slot = device(x, j - 4, z, 1), y * NC + core
            mine = (core == 1) & (y == j - 4)
        deliver(mine, sent.at[j], came.at[slot], x_send, x_recv, to)

    for step in range(1, EARLY + 1):
        ring(step)

    wait_bytes(came, x_recv)

    @pl.loop(0, outer // 8)
    def _(step):
        rows = pl.ds(pl.multiple_of(step * 8, 8), 8)
        values = [came[m, rows, :] for m in range(8)]
        for level in range(3):
            half = 1 << level
            for m in range(8):
                if not m & half:
                    first, second = values[m], values[m | half]
                    values[m], values[m | half] = first + second, first - second
        for m in range(8):
            table[m, rows, :] = values[m]

    for c in range(NC):
        for step in range(1, 4):
            to_q = (q + step) & 3
            remote(
                table.at[to_q * 2 + c], crossed.at[c, q], q_send, q_recv.at[c], by_role(p, to_q, z)
            ).start()
        pltpu.make_async_copy(table.at[q * 2 + c], crossed.at[c, q], q_recv.at[c]).start()

    for step in range(EARLY + 1, NZ // 2 + 1):
        ring(step)

    for i in range(4):
        deliver(
            role0 & (x == y) & (x == i), idx_z, idx_all.at[core, y], i_send, i_recv, device(i, x, z, 0)
        )
        deliver(
            (core == 1) & (x == y) & (y == i), idx_z, idx_all.at[core, x], i_send, i_recv, device(y, i, z, 1)
        )
    wait_bytes(idx_all, i_recv)

    sublane = lax.broadcasted_iota(jnp.int32, (8, LANES), 0)

    def fold_rows(groups):
        for level in (4, 2, 1):
            count = len(groups) // 2
            groups = [
                jnp.where(
                    (sublane & level) == 0,
                    first + pltpu.roll(first, 8 - level, 0),
                    second + pltpu.roll(second, level, 0),
                )
                for first, second in zip(groups[:count], groups[count:])
            ]
        return groups[0]

    def z_order(step):
        half = (step + 1) >> 1
        return (z + NZ // 2 + jnp.where((step & 1) == 1, half, NZ - half)) & (NZ - 1)

    for c in range(NC):
        wait_bytes(crossed.at[c], q_recv.at[c])

        @pl.loop(0, outer // 8)
        def _(step):
            rows = pl.ds(pl.multiple_of(step * 8, 8), 8)
            values = [crossed[c, m, rows, :] for m in range(4)]
            for level in range(2):
                half = 1 << level
                for m in range(4):
                    if not m & half:
                        first, second = values[m], values[m | half]
                        values[m], values[m | half] = first + second, first - second
            for m in range(4):
                came[c * 4 + m, rows, :] = values[m]

    @pl.loop(0, NZ)
    def _(step):
        to_z = z_order(step)
        found = []
        for m in range(8):
            offset = jnp.broadcast_to(idx_all[m // 4, m % 4, to_z], (8, LANES))
            lane = offset & (LANES - 1)
            key = ((offset >> 7) & (outer - 1)) - sublane
            chains = [jnp.zeros((8, LANES), jnp.float32)] * 2
            for i in range(outer // 8):
                there = jnp.take_along_axis(
                    came[m, 8 * i : 8 * i + 8, :], lane, axis=1, mode="promise_in_bounds"
                )
                chains[i & 1] = jnp.where(key == 8 * i, there, chains[i & 1])
            found.append(chains[0] + chains[1])
        pick[to_z] = fold_rows(found)

        @pl.when(step < NZ - 1)
        def _():
            remote(pick.at[to_z], zcame.at[z], z_send, z_recv, by_role(p, q, to_z)).start()

    zcame[z] = pick[z]
    wait_bytes(zcame.at[pl.ds(0, NZ - 1)], z_recv)
    total = zcame[0]
    for other in range(1, NZ):
        total = total + signed(parity(z & other, 4), zcame[other])
    total = total * scale
    for m in range(8):
        rows_out[m] = total[m : m + 1, :]
    slot = core * 4 + p
    for m in range(8):
        to_c, to_q = m // 4, m % 4
        to = device(jnp.where(role0, q, to_q), jnp.where(role0, to_q, q), z, to_c)
        mine = (core == to_c) & (p == q) & (q == to_q)
        deliver(mine, rows_out.at[m], rows_in.at[slot], r_send, r_recv, to)
    wait_bytes(rows_in, r_recv)
    for j in range(8):
        out[j : j + 1, :] = rows_in[j]

    wait_bytes(idx_z.at[pl.ds(0, NZ - 1)], ring_send)
    wait_bytes(sent.at[pl.ds(0, 7)], x_send)
    wait_bytes(sent.at[pl.ds(0, 6)], q_send)
    wait_bytes(pick.at[pl.ds(0, NZ - 1)], z_send)

    @pl.when(x == y)
    def _():
        wait_bytes(idx_all.at[0], i_send)
        wait_bytes(idx_all.at[0, pl.ds(0, 3)], i_send)
        wait_bytes(rows_out.at[pl.ds(0, 7)], r_send)

    @pl.when(x != y)
    def _():
        wait_bytes(idx_all, i_send)
        wait_bytes(rows_out, r_send)


def per_device(panel, signs, samples):
    cols, rows = panel.shape
    samp = samples.shape[0]
    n_wide, n_narrow = lax.axis_size("wide"), lax.axis_size("narrow")
    scale = 1.0 / math.sqrt(samp * n_wide * n_narrow)
    outer = rows // LANES
    dma = pltpu.SemaphoreType.DMA
    vmem = pl.BlockSpec(memory_space=pltpu.VMEM)
    hbm = pl.BlockSpec(memory_space=pl.ANY)
    f32, i32 = jnp.float32, jnp.int32
    return pl.pallas_call(
        functools.partial(kernel, scale),
        out_shape=jax.ShapeDtypeStruct((cols, samp), f32),
        in_specs=[hbm, hbm, vmem],
        out_specs=vmem,
        scratch_shapes=[
            pltpu.VMEM((cols, rows), f32),
            pltpu.VMEM((outer, LANES), i32),
            pltpu.VMEM((cols * outer, LANES), f32),
            pltpu.VMEM((8, outer, LANES), f32),
            pltpu.VMEM((8, outer, LANES), f32),
            pltpu.VMEM((8, outer, LANES), f32),
            pltpu.VMEM((NC, 4, outer, LANES), f32),
            pltpu.VMEM((NZ, 1, LANES), i32),
            pltpu.VMEM((NC, 4, NZ, 1, LANES), i32),
            pltpu.VMEM((NZ, 8, LANES), f32),
            pltpu.VMEM((NZ, 8, LANES), f32),
            pltpu.VMEM((8, 1, LANES), f32),
            pltpu.VMEM((8, 1, LANES), f32),
            dma((CHUNKS, 2)), dma, dma((NZ // 2,)), dma((NZ // 2,)), dma, dma, dma, dma((NC,)),
            dma, dma, dma, dma, dma, dma,
        ],
        compiler_params=pltpu.CompilerParams(collective_id=0, has_side_effects=True),
    )(panel, signs.reshape(outer, LANES), samples.reshape(1, samp))


def solution(mesh):
    in_specs = (P(None, ("wide", "narrow")), P(("wide", "narrow")), P(("wide", "narrow")))
    out_specs = P(None, ("wide", "narrow"))
    return jax.shard_map(
        per_device, mesh=mesh, in_specs=in_specs, out_specs=out_specs, check_vma=False
    )
```

time: 103 us -> 56.5 us (0.55)
  Pallas kernels: 101 us -> 55.1 us
    pallas_call x1, Pallas kernels: 101 us -> 55.1 us  [per_device(): pl.pallas_call(functools.partial(kernel, scale), out_shape=jax.ShapeDtype...]
where the time goes in v2:
time: 56.5 us; the launch traced here: 56.4 us
  Pallas kernels  55.1 us (98%)
  local copies, waits for them, and re-layouts  1.28 us (2%)
    pallas_call x1, Pallas kernels, per_device(): pl.pallas_call(functools.partial(kernel, scale), out_shape=jax.ShapeDtype...  55.1 us
    unnamed x1, local copies, waits for them, and re-layouts  1.28 us

profile of v2, /device:TPU:1, one launch (start us, length us, event | category | flops | bytes accessed | tf_op | source)
XLA Modules:
  0.0 56.4 jit_solution(2170241967327827678)
XLA Ops:
  0.0 55.1 %shard_map.37 = f32[8,128]{1,0:T(8,128)} custom-call(f32[8,32768]{1,0:T(8,128)} %panel_hbm.1, s32[256,128]{1,0:T(8,128)} %bitcast.2, s32[1,128]{1,0:T(1,128)} %bitcast.3), custom_call_target="tpu_custom_call" | custom-call | tf_op jit(solution)/shard_map/pallas_call | solution.py:304
  55.1 1.3 %copy.5 = f32[8,128]{1,0:T(8,128)} copy(f32[8,128]{1,0:T(8,128)} %shard_map.37) | data formatting | bytes 8192

commit v3 on v2

--- a/solution.py
+++ b/solution.py
@@ -12,7 +12,8 @@
 NX, NY, NZ, NC = 4, 4, 16, 2
 LANES = 128
 CHUNKS = 4
-EARLY = 5
+HALVES = 2
+NEAR = 4
 
 
 def parity(value, bits):
@@ -44,9 +45,9 @@
 
 def kernel(
     scale, panel_hbm, signs_hbm, samples, out,
-    panel, signs, mixed, sent, came, table, crossed, idx_z, idx_all, pick, zcame, rows_out, rows_in,
-    load_sem, ring_send, up_recv, down_recv, x_send, x_recv, q_send, q_recv,
-    i_send, i_recv, z_send, z_recv, r_send, r_recv,
+    panel, signs, mixed, sent, came, table, crossed, idx_all, pick, zcame, rows_out, rows_in,
+    load_sem, relay, x_send, x_recv, q_send, q_recv,
+    ip_send, ip_recv, iz_send, iz_recv, z_send, z_recv, r_send, r_recv,
 ):
     wide = lax.axis_index("wide")
     narrow = lax.axis_index("narrow")
@@ -98,9 +99,9 @@
     def greet(to):
         pl.semaphore_signal(barrier, inc=1, device_id=to, device_id_type=MESH)
 
-    above, below = (z + 1) & (NZ - 1), (z - 1) & (NZ - 1)
-    greet(device(x, y, above, core))
-    greet(device(x, y, below, core))
+    for step in range(1, NEAR + 1):
+        greet(device(x, y, (z + step) & (NZ - 1), core))
+        greet(device(x, y, (z - step) & (NZ - 1), core))
 
     @pl.loop(1, NX * NY * NC)
     def _(step):
@@ -123,82 +124,84 @@
         )
     h_rows = hadamard(outer, outer, outer.bit_length() - 1)
 
-    pl.semaphore_wait(barrier, NX * NY * NC + 1)
-
-    up, down = device(x, y, above, core), device(x, y, below, core)
-    idx_z[z] = samples[...]
-
-    def ring_up(step):
-        row = (z - step) & (NZ - 1)
-        src = samples if step == 0 else idx_z.at[row]
-        return remote(src, idx_z.at[row], ring_send, up_recv.at[step], up)
-
-    def ring_down(step):
-        row = (z + step) & (NZ - 1)
-        src = samples if step == 0 else idx_z.at[row]
-        return remote(src, idx_z.at[row], ring_send, down_recv.at[step], down)
-
-    def ring(step):
-        ring_up(step - 1).wait_recv()
-        if step < NZ // 2:
-            ring_up(step).start()
-            ring_down(step - 1).wait_recv()
-            if step < NZ // 2 - 1:
-                ring_down(step).start()
-
-    ring_up(0).start()
-    ring_down(0).start()
-
     for j in range(8):
         high, low = split(mixed[pl.ds(j, outer, stride=8), :])
         both = jnp.concatenate([high, low], axis=1)
         done = jnp.dot(h_rows, both, preferred_element_type=jnp.float32)
         sent[j] = done[:, :LANES] + done[:, LANES:]
-        if j < 4:
-            to, slot = device(j, y, z, 0), x * NC + core
-            mine = (core == 0) & (x == j)
-        else:
-            to, slot = device(x, j - 4, z, 1), y * NC + core
-            mine = (core == 1) & (y == j - 4)
-        deliver(mine, sent.at[j], came.at[slot], x_send, x_recv, to)
-
-    for step in range(1, EARLY + 1):
-        ring(step)
-
-    wait_bytes(came, x_recv)
-
-    @pl.loop(0, outer // 8)
-    def _(step):
-        rows = pl.ds(pl.multiple_of(step * 8, 8), 8)
-        values = [came[m, rows, :] for m in range(8)]
-        for level in range(3):
-            half = 1 << level
-            for m in range(8):
-                if not m & half:
-                    first, second = values[m], values[m | half]
-                    values[m], values[m | half] = first + second, first - second
-        for m in range(8):
-            table[m, rows, :] = values[m]
-
-    for c in range(NC):
-        for step in range(1, 4):
-            to_q = (q + step) & 3
-            remote(
-                table.at[to_q * 2 + c], crossed.at[c, q], q_send, q_recv.at[c], by_role(p, to_q, z)
-            ).start()
-        pltpu.make_async_copy(table.at[q * 2 + c], crossed.at[c, q], q_recv.at[c]).start()
-
-    for step in range(EARLY + 1, NZ // 2 + 1):
-        ring(step)
+
+    pl.semaphore_wait(barrier, NX * NY * NC - 1 + 2 * NEAR)
+
+    for side, to_z in enumerate((z + NEAR, z - NEAR)):
+        pl.semaphore_signal(
+            relay.at[side], inc=1, device_id=device(x, y, to_z & (NZ - 1), core), device_id_type=MESH
+        )
 
     for i in range(4):
         deliver(
-            role0 & (x == y) & (x == i), idx_z, idx_all.at[core, y], i_send, i_recv, device(i, x, z, 0)
+            role0 & (x == y) & (x == i), samples, idx_all.at[z, core * 4 + y], ip_send, ip_recv,
+            device(i, x, z, 0),
         )
         deliver(
-            (core == 1) & (x == y) & (y == i), idx_z, idx_all.at[core, x], i_send, i_recv, device(y, i, z, 1)
-        )
-    wait_bytes(idx_all, i_recv)
+            (core == 1) & (x == y) & (y == i), samples, idx_all.at[z, core * 4 + x], ip_send, ip_recv,
+            device(y, i, z, 1),
+        )
+
+    for half in range(HALVES):
+        rows = pl.ds(half * (outer // HALVES), outer // HALVES)
+
+        def column(j, slot):
+            return sent.at[j, rows], came.at[slot, rows]
+
+        by_x, by_y = x * NC + core, y * NC + core
+        for step in (2, 1, 3):
+            other = (x + step) & 3
+            remote(*column(other, by_x), x_send, x_recv.at[half], device(other, y, z, 0)).start()
+            other = (y + step) & 3
+            remote(*column(4 + other, by_y), x_send, x_recv.at[half], device(x, other, z, 1)).start()
+        deliver(role0, *column(x, by_x), x_send, x_recv.at[half], device(x, y, z, 0))
+        deliver(core == 1, *column(4 + y, by_y), x_send, x_recv.at[half], device(x, y, z, 1))
+
+    def z_order(step):
+        half = (step + 1) >> 1
+        return (z + NZ // 2 + jnp.where((step & 1) == 1, half, NZ - half)) & (NZ - 1)
+
+    pl.semaphore_wait(relay.at[0], 1)
+    pl.semaphore_wait(relay.at[1], 1)
+    wait_bytes(idx_all.at[0], ip_recv)
+
+    @pl.loop(0, NZ - 1)
+    def _(step):
+        remote(idx_all.at[z], idx_all.at[z], iz_send, iz_recv, by_role(p, q, z_order(step))).start()
+
+    for part in range(HALVES):
+        wait_bytes(came.at[:, pl.ds(0, outer // HALVES)], x_recv.at[part])
+
+        @pl.loop(part * (outer // 8 // HALVES), (part + 1) * (outer // 8 // HALVES))
+        def _(step):
+            rows = pl.ds(pl.multiple_of(step * 8, 8), 8)
+            values = [came[m, rows, :] for m in range(8)]
+            for level in range(3):
+                half = 1 << level
+                for m in range(8):
+                    if not m & half:
+                        first, second = values[m], values[m | half]
+                        values[m], values[m | half] = first + second, first - second
+            for m in range(8):
+                table[m, rows, :] = values[m]
+
+        rows = pl.ds(part * (outer // HALVES), outer // HALVES)
+        for step in (2, 1, 3):
+            to_q = (q + step) & 3
+            for c in range(NC):
+                remote(
+                    table.at[to_q * 2 + c, rows], crossed.at[c, q, rows], q_send, q_recv.at[part],
+                    by_role(p, to_q, z),
+                ).start()
+        for c in range(NC):
+            pltpu.make_async_copy(
+                table.at[q * 2 + c, rows], crossed.at[c, q, rows], q_recv.at[part]
+            ).start()
 
     sublane = lax.broadcasted_iota(jnp.int32, (8, LANES), 0)
 
@@ -215,32 +218,30 @@
             ]
         return groups[0]
 
-    def z_order(step):
-        half = (step + 1) >> 1
-        return (z + NZ // 2 + jnp.where((step & 1) == 1, half, NZ - half)) & (NZ - 1)
-
-    for c in range(NC):
-        wait_bytes(crossed.at[c], q_recv.at[c])
-
-        @pl.loop(0, outer // 8)
+    wait_bytes(idx_all.at[pl.ds(0, NZ - 1)], iz_recv)
+    for part in range(HALVES):
+        wait_bytes(crossed.at[:, :, pl.ds(0, outer // HALVES)], q_recv.at[part])
+
+        @pl.loop(part * (outer // 8 // HALVES), (part + 1) * (outer // 8 // HALVES))
         def _(step):
             rows = pl.ds(pl.multiple_of(step * 8, 8), 8)
-            values = [crossed[c, m, rows, :] for m in range(4)]
-            for level in range(2):
-                half = 1 << level
+            for c in range(NC):
+                values = [crossed[c, m, rows, :] for m in range(4)]
+                for level in range(2):
+                    half = 1 << level
+                    for m in range(4):
+                        if not m & half:
+                            first, second = values[m], values[m | half]
+                            values[m], values[m | half] = first + second, first - second
                 for m in range(4):
-                    if not m & half:
-                        first, second = values[m], values[m | half]
-                        values[m], values[m | half] = first + second, first - second
-            for m in range(4):
-                came[c * 4 + m, rows, :] = values[m]
+                    came[c * 4 + m, rows, :] = values[m]
 
     @pl.loop(0, NZ)
     def _(step):
         to_z = z_order(step)
         found = []
         for m in range(8):
-            offset = jnp.broadcast_to(idx_all[m // 4, m % 4, to_z], (8, LANES))
+            offset = jnp.broadcast_to(idx_all[to_z, m], (8, LANES))
             lane = offset & (LANES - 1)
             key = ((offset >> 7) & (outer - 1)) - sublane
             chains = [jnp.zeros((8, LANES), jnp.float32)] * 2
@@ -274,20 +275,19 @@
     for j in range(8):
         out[j : j + 1, :] = rows_in[j]
 
-    wait_bytes(idx_z.at[pl.ds(0, NZ - 1)], ring_send)
     wait_bytes(sent.at[pl.ds(0, 7)], x_send)
     wait_bytes(sent.at[pl.ds(0, 6)], q_send)
+    wait_bytes(idx_all.at[pl.ds(0, NZ - 1)], iz_send)
     wait_bytes(pick.at[pl.ds(0, NZ - 1)], z_send)
 
     @pl.when(x == y)
     def _():
-        wait_bytes(idx_all.at[0], i_send)
-        wait_bytes(idx_all.at[0, pl.ds(0, 3)], i_send)
+        wait_bytes(idx_all.at[0, pl.ds(0, 7)], ip_send)
         wait_bytes(rows_out.at[pl.ds(0, 7)], r_send)
 
     @pl.when(x != y)
     def _():
-        wait_bytes(idx_all, i_send)
+        wait_bytes(idx_all.at[0], ip_send)
         wait_bytes(rows_out, r_send)
 
 
@@ -304,7 +304,7 @@
     return pl.pallas_call(
         functools.partial(kernel, scale),
         out_shape=jax.ShapeDtypeStruct((cols, samp), f32),
-        in_specs=[hbm, hbm, vmem],
+        in_specs=[hbm, hbm, hbm],
         out_specs=vmem,
         scratch_shapes=[
             pltpu.VMEM((cols, rows), f32),
@@ -314,14 +314,13 @@
             pltpu.VMEM((8, outer, LANES), f32),
             pltpu.VMEM((8, outer, LANES), f32),
             pltpu.VMEM((NC, 4, outer, LANES), f32),
-            pltpu.VMEM((NZ, 1, LANES), i32),
-            pltpu.VMEM((NC, 4, NZ, 1, LANES), i32),
+            pltpu.VMEM((NZ, 8, 1, LANES), i32),
             pltpu.VMEM((NZ, 8, LANES), f32),
             pltpu.VMEM((NZ, 8, LANES), f32),
             pltpu.VMEM((8, 1, LANES), f32),
             pltpu.VMEM((8, 1, LANES), f32),
-            dma((CHUNKS, 2)), dma, dma((NZ // 2,)), dma((NZ // 2,)), dma, dma, dma, dma((NC,)),
-            dma, dma, dma, dma, dma, dma,
+            dma((CHUNKS, 2)), pltpu.SemaphoreType.REGULAR((2,)), dma, dma((HALVES,)), dma, dma((HALVES,)),
+            dma, dma, dma, dma, dma, dma, dma, dma,
         ],
         compiler_params=pltpu.CompilerParams(collective_id=0, has_side_effects=True),
     )(panel, signs.reshape(outer, LANES), samples.reshape(1, samp))

time: 56.5 us -> 45.2 us (0.80)
  Pallas kernels: 55.1 us -> 43.8 us
    pallas_call x1, Pallas kernels: 55.1 us -> 43.8 us  [per_device(): pl.pallas_call(functools.partial(kernel, scale), out_shape=jax.ShapeDtype...]
where the time goes in v3:
time: 45.2 us; the launch traced here: 45.1 us
  Pallas kernels  43.8 us (97%)
  local copies, waits for them, and re-layouts  1.28 us (3%)
    pallas_call x1, Pallas kernels, per_device(): pl.pallas_call(functools.partial(kernel, scale), out_shape=jax.ShapeDtype...  43.8 us
    unnamed x1, local copies, waits for them, and re-layouts  1.28 us

profile of v3, /device:TPU:1, one launch (start us, length us, event | category | flops | bytes accessed | tf_op | source)
XLA Modules:
  0.0 45.1 jit_solution(16744557370252241893)
XLA Ops:
  0.0 43.8 %shard_map.37 = f32[8,128]{1,0:T(8,128)} custom-call(f32[8,32768]{1,0:T(8,128)} %panel_hbm.1, s32[256,128]{1,0:T(8,128)} %bitcast.2, s32[1,128]{1,0:T(1,128)} %bitcast.3), custom_call_target="tpu_custom_call" | custom-call | tf_op jit(solution)/shard_map/pallas_call | solution.py:304
  43.8 1.3 %copy.5 = f32[8,128]{1,0:T(8,128)} copy(f32[8,128]{1,0:T(8,128)} %shard_map.37) | data formatting | bytes 8192

commit v4 on v3

--- a/solution.py
+++ b/solution.py
@@ -45,9 +45,9 @@
 
 def kernel(
     scale, panel_hbm, signs_hbm, samples, out,
-    panel, signs, mixed, sent, came, table, crossed, idx_all, pick, zcame, rows_out, rows_in,
+    panel, signs, mixed, sent, came, table, crossed, idx_all, pick, zcame,
     load_sem, relay, x_send, x_recv, q_send, q_recv,
-    ip_send, ip_recv, iz_send, iz_recv, z_send, z_recv, r_send, r_recv,
+    ip_send, ip_recv, iz_send, iz_recv, z_send, z_recv,
 ):
     wide = lax.axis_index("wide")
     narrow = lax.axis_index("narrow")
@@ -236,59 +236,67 @@
                 for m in range(4):
                     came[c * 4 + m, rows, :] = values[m]
 
-    @pl.loop(0, NZ)
-    def _(step):
-        to_z = z_order(step)
+    def choose(to_z):
         found = []
         for m in range(8):
             offset = jnp.broadcast_to(idx_all[to_z, m], (8, LANES))
             lane = offset & (LANES - 1)
-            key = ((offset >> 7) & (outer - 1)) - sublane
-            chains = [jnp.zeros((8, LANES), jnp.float32)] * 2
+            row = offset >> 7
+            bits = [(row & (8 << level)) != 0 for level in range((outer // 8).bit_length() - 1)]
+            waiting = []
             for i in range(outer // 8):
                 there = jnp.take_along_axis(
                     came[m, 8 * i : 8 * i + 8, :], lane, axis=1, mode="promise_in_bounds"
                 )
-                chains[i & 1] = jnp.where(key == 8 * i, there, chains[i & 1])
-            found.append(chains[0] + chains[1])
-        pick[to_z] = fold_rows(found)
-
-        @pl.when(step < NZ - 1)
-        def _():
-            remote(pick.at[to_z], zcame.at[z], z_send, z_recv, by_role(p, q, to_z)).start()
-
-    zcame[z] = pick[z]
-    wait_bytes(zcame.at[pl.ds(0, NZ - 1)], z_recv)
-    total = zcame[0]
-    for other in range(1, NZ):
-        total = total + signed(parity(z & other, 4), zcame[other])
-    total = total * scale
+                level = 0
+                while waiting and waiting[-1][0] == level:
+                    there = jnp.where(bits[level], there, waiting.pop()[1])
+                    level += 1
+                waiting.append((level, there))
+            found.append(jnp.where((row & 7) == sublane, waiting[0][1], 0.0))
+        rows = fold_rows(found)
+        for m in range(8):
+            pick[to_z, m] = rows[m : m + 1, :]
+
+    slot = core * 4 + p
+
+    def owner(m, to_z):
+        to_c, to_q = m // 4, m % 4
+        return device(jnp.where(role0, q, to_q), jnp.where(role0, to_q, q), to_z, to_c)
+
+    @pl.loop(0, NZ - 1)
+    def _(step):
+        to_z = z_order(step)
+        choose(to_z)
+        for m in range(8):
+            remote(pick.at[to_z, m], zcame.at[z, slot], z_send, z_recv, owner(m, to_z)).start()
+
+    choose(z)
     for m in range(8):
-        rows_out[m] = total[m : m + 1, :]
-    slot = core * 4 + p
-    for m in range(8):
-        to_c, to_q = m // 4, m % 4
-        to = device(jnp.where(role0, q, to_q), jnp.where(role0, to_q, q), z, to_c)
-        mine = (core == to_c) & (p == q) & (q == to_q)
-        deliver(mine, rows_out.at[m], rows_in.at[slot], r_send, r_recv, to)
-    wait_bytes(rows_in, r_recv)
+        mine = (core == m // 4) & (p == q) & (q == m % 4)
+        deliver(mine, pick.at[z, m], zcame.at[z, slot], z_send, z_recv, owner(m, z))
+
+    wait_bytes(zcame, z_recv)
     for j in range(8):
-        out[j : j + 1, :] = rows_in[j]
+        total = zcame[0, j]
+        for other in range(1, NZ):
+            total = total + signed(parity(z & other, 4), zcame[other, j])
+        out[j : j + 1, :] = total * scale
 
     wait_bytes(sent.at[pl.ds(0, 7)], x_send)
     wait_bytes(sent.at[pl.ds(0, 6)], q_send)
     wait_bytes(idx_all.at[pl.ds(0, NZ - 1)], iz_send)
-    wait_bytes(pick.at[pl.ds(0, NZ - 1)], z_send)
 
     @pl.when(x == y)
     def _():
         wait_bytes(idx_all.at[0, pl.ds(0, 7)], ip_send)
-        wait_bytes(rows_out.at[pl.ds(0, 7)], r_send)
+        wait_bytes(pick.at[pl.ds(0, NZ - 1)], z_send)
+        wait_bytes(pick.at[0, pl.ds(0, 7)], z_send)
 
     @pl.when(x != y)
     def _():
         wait_bytes(idx_all.at[0], ip_send)
-        wait_bytes(rows_out, r_send)
+        wait_bytes(pick, z_send)
 
 
 def per_device(panel, signs, samples):
@@ -315,12 +323,10 @@
             pltpu.VMEM((8, outer, LANES), f32),
             pltpu.VMEM((NC, 4, outer, LANES), f32),
             pltpu.VMEM((NZ, 8, 1, LANES), i32),
-            pltpu.VMEM((NZ, 8, LANES), f32),
-            pltpu.VMEM((NZ, 8, LANES), f32),
-            pltpu.VMEM((8, 1, LANES), f32),
-            pltpu.VMEM((8, 1, LANES), f32),
+            pltpu.VMEM((NZ, 8, 1, LANES), f32),
+            pltpu.VMEM((NZ, 8, 1, LANES), f32),
             dma((CHUNKS, 2)), pltpu.SemaphoreType.REGULAR((2,)), dma, dma((HALVES,)), dma, dma((HALVES,)),
-            dma, dma, dma, dma, dma, dma, dma, dma,
+            dma, dma, dma, dma, dma, dma,
         ],
         compiler_params=pltpu.CompilerParams(collective_id=0, has_side_effects=True),
     )(panel, signs.reshape(outer, LANES), samples.reshape(1, samp))

time: 45.2 us -> 43.6 us (0.965)
  Pallas kernels: 43.8 us -> 42.1 us
    pallas_call x1, Pallas kernels: 43.8 us -> 42.1 us  [per_device(): pl.pallas_call(functools.partial(kernel, scale), out_shape=jax.ShapeDtype...]
where the time goes in v4:
time: 43.6 us; the launch traced here: 43.4 us
  Pallas kernels  42.1 us (97%)
  local copies, waits for them, and re-layouts  1.28 us (3%)
    pallas_call x1, Pallas kernels, per_device(): pl.pallas_call(functools.partial(kernel, scale), out_shape=jax.ShapeDtype...  42.1 us
    unnamed x1, local copies, waits for them, and re-layouts  1.28 us

profile of v4, /device:TPU:1, one launch (start us, length us, event | category | flops | bytes accessed | tf_op | source)
XLA Modules:
  0.0 43.4 jit_solution(15187283702138417421)
XLA Ops:
  0.0 42.1 %shard_map.37 = f32[8,128]{1,0:T(8,128)} custom-call(f32[8,32768]{1,0:T(8,128)} %panel_hbm.1, s32[256,128]{1,0:T(8,128)} %bitcast.2, s32[1,128]{1,0:T(1,128)} %bitcast.3), custom_call_target="tpu_custom_call" | custom-call | tf_op jit(solution)/shard_map/pallas_call | solution.py:312
  42.1 1.3 %copy.5 = f32[8,128]{1,0:T(8,128)} copy(f32[8,128]{1,0:T(8,128)} %shard_map.37) | data formatting | bytes 8192

commit v5 on v4

--- a/solution.py
+++ b/solution.py
@@ -11,8 +11,8 @@
 MESH = pl.DeviceIdType.MESH
 NX, NY, NZ, NC = 4, 4, 16, 2
 LANES = 128
-CHUNKS = 4
-HALVES = 2
+CHUNKS = 2
+PARTS = 4
 NEAR = 4
 
 
@@ -147,8 +147,8 @@
             device(y, i, z, 1),
         )
 
-    for half in range(HALVES):
-        rows = pl.ds(half * (outer // HALVES), outer // HALVES)
+    for half in range(PARTS):
+        rows = pl.ds(half * (outer // PARTS), outer // PARTS)
 
         def column(j, slot):
             return sent.at[j, rows], came.at[slot, rows]
@@ -174,10 +174,10 @@
     def _(step):
         remote(idx_all.at[z], idx_all.at[z], iz_send, iz_recv, by_role(p, q, z_order(step))).start()
 
-    for part in range(HALVES):
-        wait_bytes(came.at[:, pl.ds(0, outer // HALVES)], x_recv.at[part])
-
-        @pl.loop(part * (outer // 8 // HALVES), (part + 1) * (outer // 8 // HALVES))
+    for part in range(PARTS):
+        wait_bytes(came.at[:, pl.ds(0, outer // PARTS)], x_recv.at[part])
+
+        @pl.loop(part * (outer // 8 // PARTS), (part + 1) * (outer // 8 // PARTS))
         def _(step):
             rows = pl.ds(pl.multiple_of(step * 8, 8), 8)
             values = [came[m, rows, :] for m in range(8)]
@@ -190,7 +190,7 @@
             for m in range(8):
                 table[m, rows, :] = values[m]
 
-        rows = pl.ds(part * (outer // HALVES), outer // HALVES)
+        rows = pl.ds(part * (outer // PARTS), outer // PARTS)
         for step in (2, 1, 3):
             to_q = (q + step) & 3
             for c in range(NC):
@@ -219,10 +219,10 @@
         return groups[0]
 
     wait_bytes(idx_all.at[pl.ds(0, NZ - 1)], iz_recv)
-    for part in range(HALVES):
-        wait_bytes(crossed.at[:, :, pl.ds(0, outer // HALVES)], q_recv.at[part])
-
-        @pl.loop(part * (outer // 8 // HALVES), (part + 1) * (outer // 8 // HALVES))
+    for part in range(PARTS):
+        wait_bytes(crossed.at[:, :, pl.ds(0, outer // PARTS)], q_recv.at[part])
+
+        @pl.loop(part * (outer // 8 // PARTS), (part + 1) * (outer // 8 // PARTS))
         def _(step):
             rows = pl.ds(pl.multiple_of(step * 8, 8), 8)
             for c in range(NC):
@@ -325,7 +325,7 @@
             pltpu.VMEM((NZ, 8, 1, LANES), i32),
             pltpu.VMEM((NZ, 8, 1, LANES), f32),
             pltpu.VMEM((NZ, 8, 1, LANES), f32),
-            dma((CHUNKS, 2)), pltpu.SemaphoreType.REGULAR((2,)), dma, dma((HALVES,)), dma, dma((HALVES,)),
+            dma((CHUNKS, 2)), pltpu.SemaphoreType.REGULAR((2,)), dma, dma((PARTS,)), dma, dma((PARTS,)),
             dma, dma, dma, dma, dma, dma,
         ],
         compiler_params=pltpu.CompilerParams(collective_id=0, has_side_effects=True),

time: 43.6 us -> 42.2 us (0.968)
  Pallas kernels: 42.1 us -> 40.8 us
    pallas_call x1, Pallas kernels: 42.1 us -> 40.8 us  [per_device(): pl.pallas_call(functools.partial(kernel, scale), out_shape=jax.ShapeDtype...]
where the time goes in v5:
time: 42.2 us; the launch traced here: 42.1 us
  Pallas kernels  40.8 us (97%)
  local copies, waits for them, and re-layouts  1.28 us (3%)
    pallas_call x1, Pallas kernels, per_device(): pl.pallas_call(functools.partial(kernel, scale), out_shape=jax.ShapeDtype...  40.8 us
    unnamed x1, local copies, waits for them, and re-layouts  1.28 us

profile of v5, /device:TPU:1, one launch (start us, length us, event | category | flops | bytes accessed | tf_op | source)
XLA Modules:
  0.0 42.1 jit_solution(5961754920458173792)
XLA Ops:
  0.0 40.8 %shard_map.37 = f32[8,128]{1,0:T(8,128)} custom-call(f32[8,32768]{1,0:T(8,128)} %panel_hbm.1, s32[256,128]{1,0:T(8,128)} %bitcast.2, s32[1,128]{1,0:T(1,128)} %bitcast.3), custom_call_target="tpu_custom_call" | custom-call | tf_op jit(solution)/shard_map/pallas_call | solution.py:312
  40.8 1.3 %copy.5 = f32[8,128]{1,0:T(8,128)} copy(f32[8,128]{1,0:T(8,128)} %shard_map.37) | data formatting | bytes 8192

commit v6 on v5

--- a/solution.py
+++ b/solution.py
@@ -1,4 +1,3 @@
-import functools
 import math
 
 import jax
@@ -44,7 +43,7 @@
 
 
 def kernel(
-    scale, panel_hbm, signs_hbm, samples, out,
+    panel_hbm, signs_hbm, samples, out,
     panel, signs, mixed, sent, came, table, crossed, idx_all, pick, zcame,
     load_sem, relay, x_send, x_recv, q_send, q_recv,
     ip_send, ip_recv, iz_send, iz_recv, z_send, z_recv,
@@ -281,7 +280,7 @@
         total = zcame[0, j]
         for other in range(1, NZ):
             total = total + signed(parity(z & other, 4), zcame[other, j])
-        out[j : j + 1, :] = total * scale
+        out[j : j + 1, :] = total
 
     wait_bytes(sent.at[pl.ds(0, 7)], x_send)
     wait_bytes(sent.at[pl.ds(0, 6)], q_send)
@@ -309,9 +308,9 @@
     vmem = pl.BlockSpec(memory_space=pltpu.VMEM)
     hbm = pl.BlockSpec(memory_space=pl.ANY)
     f32, i32 = jnp.float32, jnp.int32
-    return pl.pallas_call(
-        functools.partial(kernel, scale),
-        out_shape=jax.ShapeDtypeStruct((cols, samp), f32),
+    picked = pl.pallas_call(
+        kernel,
+        out_shape=pltpu.VMEM((cols, samp), f32),
         in_specs=[hbm, hbm, hbm],
         out_specs=vmem,
         scratch_shapes=[
@@ -330,6 +329,7 @@
         ],
         compiler_params=pltpu.CompilerParams(collective_id=0, has_side_effects=True),
     )(panel, signs.reshape(outer, LANES), samples.reshape(1, samp))
+    return picked * jnp.float32(scale)
 
 
 def solution(mesh):

time: 42.2 us -> 40.9 us (0.969)
  local copies, waits for them, and re-layouts: 1.28 us -> 0 us
  other arithmetic: 0 us -> 0.6 us
  Pallas kernels: 40.8 us -> 40.2 us
    unnamed x1 -> x0, local copies, waits for them, and re-layouts: 1.28 us -> none
    mul x0 -> x1, other arithmetic: none -> 0.6 us  [per_device(): return picked * jnp.float32(scale)]
    pallas_call x1, Pallas kernels: 40.8 us -> 40.2 us  [per_device(): pl.pallas_call(kernel, out_shape=pltpu.VMEM((cols, samp), f32), in_specs=...]
where the time goes in v6:
time: 40.9 us; the launch traced here: 40.8 us
  Pallas kernels  40.2 us (98%)
  other arithmetic  0.6 us (1%)
    pallas_call x1, Pallas kernels, per_device(): pl.pallas_call(kernel, out_shape=pltpu.VMEM((cols, samp), f32), in_specs=...  40.2 us

profile of v6, /device:TPU:1, one launch (start us, length us, event | category | flops | bytes accessed | tf_op | source)
XLA Modules:
  0.0 40.8 jit_solution(568525391435224900)
XLA Ops:
  0.0 40.2 %shard_map.37 = f32[8,128]{1,0:T(8,128)S(1)} custom-call(f32[8,32768]{1,0:T(8,128)} %panel_hbm.1, s32[256,128]{1,0:T(8,128)} %bitcast.2, s32[1,128]{1,0:T(1,128)} %bitcast.3), custom_call_target="tpu_custom_call" | custom-call | tf_op jit(solution)/shard_map/pallas_call | solution.py:311
  40.2 0.6 %broadcast_multiply_fusion = f32[8,128]{1,0:T(8,128)} fusion(f32[8,128]{1,0:T(8,128)S(1)} %shard_map.37), kind=kLoop, calls=%fused_computation | loop fusion | flops 1024 | bytes 8192 | tf_op jit(solution)/shard_map/mul | solution.py:332

commit v7 on v6

--- a/solution.py
+++ b/solution.py
@@ -89,18 +89,18 @@
             pltpu.make_async_copy(signs_hbm.at[rows], signs.at[rows], load_sem.at[chunk, 1]),
         )
 
+    barrier = pltpu.get_barrier_semaphore()
+
+    def greet(to):
+        pl.semaphore_signal(barrier, inc=1, device_id=to, device_id_type=MESH)
+
+    for step in range(NEAR, 0, -1):
+        greet(device(x, y, (z + step) & (NZ - 1), core))
+        greet(device(x, y, (z - step) & (NZ - 1), core))
+
     for chunk in range(CHUNKS):
         for load in loads(chunk):
             load.start()
-
-    barrier = pltpu.get_barrier_semaphore()
-
-    def greet(to):
-        pl.semaphore_signal(barrier, inc=1, device_id=to, device_id_type=MESH)
-
-    for step in range(1, NEAR + 1):
-        greet(device(x, y, (z + step) & (NZ - 1), core))
-        greet(device(x, y, (z - step) & (NZ - 1), core))
 
     @pl.loop(1, NX * NY * NC)
     def _(step):

time: 40.9 us -> 40.9 us (level)
  no operation moved by 1% of the time
where the time goes in v7:
time: 40.9 us; the launch traced here: 40.7 us
  Pallas kernels  40.1 us (98%)
  other arithmetic  0.6 us (1%)
    pallas_call x1, Pallas kernels, per_device(): pl.pallas_call(kernel, out_shape=pltpu.VMEM((cols, samp), f32), in_specs=...  40.1 us

profile of v7, /device:TPU:1, one launch (start us, length us, event | category | flops | bytes accessed | tf_op | source)
XLA Modules:
  0.0 40.7 jit_solution(6281091011298776507)
XLA Ops:
  0.0 40.1 %shard_map.37 = f32[8,128]{1,0:T(8,128)S(1)} custom-call(f32[8,32768]{1,0:T(8,128)} %panel_hbm.1, s32[256,128]{1,0:T(8,128)} %bitcast.2, s32[1,128]{1,0:T(1,128)} %bitcast.3), custom_call_target="tpu_custom_call" | custom-call | tf_op jit(solution)/shard_map/pallas_call | solution.py:311
  40.1 0.6 %broadcast_multiply_fusion = f32[8,128]{1,0:T(8,128)} fusion(f32[8,128]{1,0:T(8,128)S(1)} %shard_map.37), kind=kLoop, calls=%fused_computation | loop fusion | flops 1024 | bytes 8192 | tf_op jit(solution)/shard_map/mul | solution.py:332

commit v8 on v6

--- a/solution.py
+++ b/solution.py
@@ -10,7 +10,7 @@
 MESH = pl.DeviceIdType.MESH
 NX, NY, NZ, NC = 4, 4, 16, 2
 LANES = 128
-CHUNKS = 2
+CHUNKS = 1
 PARTS = 4
 NEAR = 4
 

time: 40.9 us -> 40.9 us (level)
  no operation moved by 1% of the time
where the time goes in v8:
time: 40.9 us; the launch traced here: 40.8 us
  Pallas kernels  40.2 us (98%)
  other arithmetic  0.6 us (1%)
    pallas_call x1, Pallas kernels, per_device(): pl.pallas_call(kernel, out_shape=pltpu.VMEM((cols, samp), f32), in_specs=...  40.2 us

profile of v8, /device:TPU:1, one launch (start us, length us, event | category | flops | bytes accessed | tf_op | source)
XLA Modules:
  0.0 40.8 jit_solution(17258098211477779055)
XLA Ops:
  0.0 40.2 %shard_map.37 = f32[8,128]{1,0:T(8,128)S(1)} custom-call(f32[8,32768]{1,0:T(8,128)} %panel_hbm.1, s32[256,128]{1,0:T(8,128)} %bitcast.2, s32[1,128]{1,0:T(1,128)} %bitcast.3), custom_call_target="tpu_custom_call" | custom-call | tf_op jit(solution)/shard_map/pallas_call | solution.py:311
  40.2 0.6 %broadcast_multiply_fusion = f32[8,128]{1,0:T(8,128)} fusion(f32[8,128]{1,0:T(8,128)S(1)} %shard_map.37), kind=kLoop, calls=%fused_computation | loop fusion | flops 1024 | bytes 8192 | tf_op jit(solution)/shard_map/mul | solution.py:332
